TPU v7x, 256 devices: a whole 4x4x8 slice. The times are simulated.
256 devices in a mesh: req: 32 (over z, y), head: 8 (over x, core).
Axes of the slice: x: 4, y: 4, z: 8, core: 2. Of those that a mesh axis runs over, the one named last changes fastest.
Arguments:
- hidden: bfloat16 [512, 2048], P('req'), may hold values from -6 to 6
- deal_order: int32 [512], replicated, may hold values from 0 to 511, each once
- lengths: int32 [512], replicated, may hold values from 1 to 8192, as said below
- page_table: int32 [512, 64], replicated, may hold values from 0 to 2047, as said below
- key_cache: bfloat16 [2048, 128, 8, 128], P('req', None, 'head'), as said below
- value_cache: bfloat16 [2048, 128, 8, 128], P('req', None, 'head'), may hold values from -12 to 12
- attn_gain: float32 [2048], replicated, may hold values from 0.1 to 1.9
- w_query: bfloat16 [2048, 2048], P(None, 'head'), may hold values from -0.125 to 0.125
- w_key: bfloat16 [2048, 1024], P(None, 'head'), may hold values from -0.125 to 0.125
- w_value: bfloat16 [2048, 1024], P(None, 'head'), may hold values from -0.125 to 0.125
- w_gate: bfloat16 [2048, 2048], P(None, 'head'), may hold values from -0.125 to 0.125
- w_out: bfloat16 [2048, 2048], P('head'), may hold values from -1.5 to 1.5
- query_gain: float32 [128], replicated, may hold values from 0.5 to 2
- key_gain: float32 [128], replicated, may hold values from 0.5 to 2
- mlp_gain: float32 [2048], replicated, may hold values from 0.1 to 1.9
- mlp_gate: bfloat16 [2048, 3072], P(None, 'head'), may hold values from -0.125 to 0.125
- mlp_up: bfloat16 [2048, 3072], P(None, 'head'), may hold values from -0.125 to 0.125
- mlp_down: bfloat16 [3072, 2048], P('head'), may hold values from -0.109375 to 0.109375
Outputs:
- output: bfloat16 [512, 2048], P('req')
Inputs may be any that keep to these rules, and one draw needn't show every extreme that they name: `lengths`: one request holds exactly 8192 cached tokens, and all requests together fill at most 2048 pages of 128 tokens. `page_table`: for request r the first ceil(lengths[r] / 128) entries of row r name, in order, the pages that hold its cached tokens; no page is named by two such entries; the other entries are arbitrary page numbers. `key_cache`: cached keys; entries lie within -402 and 402.
All inputs are finite; a program needn't handle non-finite values.
Results may differ from a plain program's by a relative error of at most 0.022.
Values may be sent and summed in bfloat16 or wider, within the bound.
A program may use at most 64 MiB of HBM per device.

v0:
```python
import math
import jax
import jax.numpy as jnp
from jax import lax
from jax.sharding import PartitionSpec as P

EPSILON = 1e-06
ROPE_BASE = 1000000.0
LOW_SCORE = -1e30
LOG_TWO = math.log(2.0)


def rms_inv(values):
    return lax.rsqrt(jnp.mean(values * values, axis=-1, keepdims=True) + EPSILON)


def rotate(values, position):
    half_dim = values.shape[-1] // 2
    exponent = jnp.arange(half_dim, dtype=jnp.float32) * (2.0 / values.shape[-1])
    frequency = ROPE_BASE ** (-exponent)
    angles = position[:, None] * frequency[None, :]
    ones_tail = (1,) * (values.ndim - 2)
    angles = angles.reshape((angles.shape[0],) + ones_tail + (half_dim,))
    cosine = jnp.cos(angles)
    sine_vals = jnp.sin(angles)
    front_half = values[..., :half_dim]
    back_half = values[..., half_dim:]
    return jnp.concatenate(
        [front_half * cosine - back_half * sine_vals, back_half * cosine + front_half * sine_vals],
        axis=-1,
    )


def norm_rotate(values, gain_vec, position):
    return rotate(values * rms_inv(values) * gain_vec, position)


def pick_rows(wanted, shard_rows):
    targets = jnp.arange(shard_rows.shape[0], dtype=jnp.int32)
    selector = (wanted[:, None] == targets[None, :]).astype(jnp.bfloat16)
    return jnp.dot(selector, shard_rows, preferred_element_type=jnp.float32)


def body(
    hidden,
    deal_order,
    lengths,
    page_table,
    key_cache,
    value_cache,
    attn_gain,
    w_query,
    w_key,
    w_value,
    w_gate,
    w_out,
    query_gain,
    key_gain,
    mlp_gain,
    mlp_gate,
    mlp_up,
    mlp_down,
):
    local_rows, model_width = hidden.shape
    req_devices = lax.axis_size("req")
    req_index = lax.axis_index("req")
    all_rows = local_rows * req_devices
    head_width = query_gain.shape[0]
    pool_pages = key_cache.shape[0]
    page_size = key_cache.shape[1]
    local_kv = key_cache.shape[2]
    group_size = w_query.shape[1] // (local_kv * head_width)
    scale_factor = 1.0 / math.sqrt(head_width)
    first_own = req_index * local_rows
    hidden_f = hidden.astype(jnp.float32)
    normed = (hidden_f * rms_inv(hidden_f) * attn_gain).astype(jnp.bfloat16)
    own_requests = lax.dynamic_slice_in_dim(deal_order, first_own, local_rows)
    position = lengths[own_requests].astype(jnp.float32)
    queries = jnp.dot(normed, w_query, preferred_element_type=jnp.float32).reshape(
        local_rows, local_kv, group_size, head_width
    )
    queries = norm_rotate(queries, query_gain, position).astype(jnp.bfloat16)
    new_keys = jnp.dot(normed, w_key, preferred_element_type=jnp.float32).reshape(
        local_rows, local_kv, head_width
    )
    new_keys = norm_rotate(new_keys, key_gain, position).astype(jnp.bfloat16)
    new_values = (
        jnp.dot(normed, w_value, preferred_element_type=jnp.float32)
        .astype(jnp.bfloat16)
        .reshape(local_rows, local_kv, head_width)
    )
    gate_logits = jnp.dot(normed, w_gate, preferred_element_type=jnp.float32)
    all_queries = lax.all_gather(queries, "req", axis=0, tiled=True)
    dealt_lengths = lengths[deal_order]
    dealt_tables = page_table[deal_order]
    page_counts = (dealt_lengths + page_size - 1) // page_size
    slot_ids = jnp.arange(dealt_tables.shape[1], dtype=jnp.int32)
    local_ids = dealt_tables - req_index * pool_pages
    usable = (
        (slot_ids[None, :] < page_counts[:, None]) & (local_ids >= 0) & (local_ids < pool_pages)
    )
    targets = jnp.where(usable, local_ids, pool_pages).reshape(-1)
    request_ids = jnp.broadcast_to(
        jnp.arange(all_rows, dtype=jnp.int32)[:, None], dealt_tables.shape
    ).reshape(-1)
    slot_flat = jnp.broadcast_to(slot_ids[None, :], dealt_tables.shape).reshape(-1)
    owners = jnp.full((pool_pages,), all_rows, jnp.int32).at[targets].set(request_ids, mode="drop")
    owner_slots = jnp.zeros((pool_pages,), jnp.int32).at[targets].set(slot_flat, mode="drop")
    safe_owners = jnp.minimum(owners, all_rows - 1)
    filled = jnp.where(
        owners < all_rows,
        jnp.clip(dealt_lengths[safe_owners] - owner_slots * page_size, 0, page_size),
        0,
    )
    page_queries = all_queries[safe_owners]
    scores = (
        jnp.einsum("pkgd,ptkd->pkgt", page_queries, key_cache, preferred_element_type=jnp.float32)
        * scale_factor
    )
    live_mask = (
        jnp.arange(page_size, dtype=jnp.int32)[None, None, None, :] < filled[:, None, None, None]
    )
    scores = jnp.where(live_mask, scores, LOW_SCORE)
    page_peaks = jnp.max(scores, axis=-1)
    local_peaks = (
        jnp.full((all_rows, local_kv, group_size), LOW_SCORE, jnp.float32)
        .at[owners]
        .max(page_peaks, mode="drop")
    )
    self_scores = (
        jnp.einsum("rkgd,rkd->rkg", queries, new_keys, preferred_element_type=jnp.float32)
        * scale_factor
    )
    own_peaks = jnp.maximum(
        lax.dynamic_slice_in_dim(local_peaks, first_own, local_rows), self_scores
    )
    with_self = lax.dynamic_update_slice_in_dim(local_peaks, own_peaks, first_own, 0)
    global_peaks = lax.pmax(with_self, "req")
    global_shift = LOG_TWO * jnp.ceil(global_peaks / LOG_TWO)
    weights = jnp.where(live_mask, jnp.exp(scores - global_shift[safe_owners][..., None]), 0.0)
    totals = (
        jnp.zeros((all_rows, local_kv, group_size), jnp.float32)
        .at[owners]
        .add(jnp.sum(weights, axis=-1), mode="drop")
    )
    page_numerators = jnp.einsum(
        "pkgt,ptkd->pkgd",
        weights.astype(jnp.bfloat16),
        value_cache,
        preferred_element_type=jnp.float32,
    )
    numerators = (
        jnp.zeros((all_rows, local_kv, group_size, head_width), jnp.float32)
        .at[owners]
        .add(page_numerators, mode="drop")
    )
    totals, numerators = (totals, numerators)
    own_totals, own_numerators = (
        lax.psum_scatter(totals, "req", scatter_dimension=0, tiled=True),
        lax.psum_scatter(numerators, "req", scatter_dimension=0, tiled=True),
    )
    own_shift = lax.dynamic_slice_in_dim(global_shift, first_own, local_rows)
    self_weight = jnp.exp(self_scores - own_shift)
    own_totals = own_totals + self_weight
    self_rounded = lax.optimization_barrier(self_weight.astype(jnp.bfloat16)).astype(jnp.float32)
    own_numerators = (
        own_numerators + self_rounded[..., None] * new_values.astype(jnp.float32)[:, :, None, :]
    )
    heads_out = (own_numerators / own_totals[..., None]).reshape(
        local_rows, local_kv * group_size * head_width
    )
    attended = (heads_out * jax.nn.sigmoid(gate_logits)).astype(jnp.bfloat16)
    projected = jnp.dot(attended, w_out, preferred_element_type=jnp.float32)
    attn_total = lax.psum(projected.astype(jnp.bfloat16), "head").astype(jnp.float32)
    mixed_rows = (hidden_f + attn_total).astype(jnp.bfloat16)
    mixed_f = mixed_rows.astype(jnp.float32)
    normed_two = (mixed_f * rms_inv(mixed_f) * mlp_gain).astype(jnp.bfloat16)
    gate_part = jnp.dot(normed_two, mlp_gate, preferred_element_type=jnp.float32)
    up_part = jnp.dot(normed_two, mlp_up, preferred_element_type=jnp.float32)
    inner_act = (jax.nn.silu(gate_part) * up_part).astype(jnp.bfloat16)
    down_part = jnp.dot(inner_act, mlp_down, preferred_element_type=jnp.float32)
    inverse_order = (
        jnp.zeros((all_rows,), jnp.int32).at[deal_order].set(jnp.arange(all_rows, dtype=jnp.int32))
    )
    wanted = lax.dynamic_slice_in_dim(inverse_order, first_own, local_rows)
    mlp_total = lax.psum(down_part.astype(jnp.bfloat16), "head").astype(jnp.float32)
    result = (mixed_f + mlp_total).astype(jnp.bfloat16)
    gathered = pick_rows(wanted, lax.all_gather(result, "req", axis=0, tiled=True))
    output = gathered.astype(jnp.bfloat16)
    return output


def solution(mesh):
    return jax.shard_map(
        body,
        mesh=mesh,
        in_specs=(
            P("req", None),
            P(),
            P(),
            P(),
            P("req", None, "head", None),
            P("req", None, "head", None),
            P(),
            P(None, "head"),
            P(None, "head"),
            P(None, "head"),
            P(None, "head"),
            P("head", None),
            P(),
            P(),
            P(),
            P(None, "head"),
            P(None, "head"),
            P("head", None),
        ),
        out_specs=P("req", None),
        check_vma=False,
    )
```

profile of v0, /device:TPU:2, one launch (start us, length us, event | category | flops | bytes accessed | tf_op | source)
XLA Modules:
  0.0 1038.4 jit_solution(14262938876819041306)
XLA Ops:
  6.6 0.8 compare_select_fusion.1
  7.5 0.8 compare_select_fusion.2
  8.3 1.0 fusion.17
  9.3 3.6 gather_fusion
  12.9 0.7 gather_fusion.3
  13.6 0.3 fusion.77
  13.9 0.1 multiply_reduce_fusion
  14.0 0.1 iota_compare_fusion
  14.2 0.1 lt.102
  14.3 0.1 multiply_cosine_fusion.1
  14.5 0.1 multiply_multiply_fusion
  14.6 0.1 subtract_convert_fusion
  14.6 0.1 pad_maximum_fusion
  14.7 52.5 %all_gather.6 = bf16[512,1,2,128]{3,2,1,0:T(2,128)(2,1)S(1)} all-gather(bf16[16,1,2,128]{3,2,1,0:T(2,128)(2,1)S(1)} %pad_maximum_fusion), channel_id=1, replica_groups=mesh['req'=32,'head'=8] {'req'}, dimensions={0}, use_global_device_ids=true | all-gather | bytes 270336 | tf_op jit(solution)/shard_map/all_gather | solution.py:93
  67.2 0.1 copy.63
  67.3 1.0 gather_fusion.1
  68.4 0.2 sub.57
  68.6 0.1 reshape.511
  68.8 0.1 reshape.503
  68.9 0.4 compare_select_fusion
  69.3 120.0 %scatter_custom_fusion.2 = s32[64]{0:T(128)S(1)} fusion(s32[32768]{0:T(1024)S(1)} %bitcast.102, s32[32768]{0:T(1024)S(1)} %reshape.511, s32[]{:T(128)} %constant.24.clone.1), kind=kCustom, calls=%fused_computation.126 | custom fusion | bytes 260 | tf_op jit(solution)/shard_map/scatter | solution.py:108
  189.3 120.0 %scatter_custom_fusion.1 = s32[64]{0:T(128)S(1)} fusion(s32[32768]{0:T(1024)S(1)} %bitcast.103, s32[32768]{0:T(1024)S(1)} %reshape.503, s32[]{:T(128)} %constant.25.clone.1), kind=kCustom, calls=%fused_computation.128 | custom fusion | bytes 260 | tf_op jit(solution)/shard_map/scatter | solution.py:107
  309.4 0.8 gather_fusion.2
  310.2 0.6 gather_fusion.4
  310.8 0.1 iota_compare_fusion.1
  310.9 1.3 fusion.80
  312.2 0.9 scatter_custom_fusion.3
  313.1 0.1 copy.66
  313.2 0.4 multiply_reduce_fusion.1
  313.7 0.1 fusion.56
  313.8 0.1 maximum_bitcast_fusion
  313.9 0.2 fusion.53
  314.1 0.1 copy.73
  314.1 0.1 copy.67
  314.2 0.1 dynamic_update_slice.3
  314.4 72.4 %pmax.7 = f32[512,1,2]{0,2,1:T(2,128)S(1)} all-reduce(f32[512,1,2]{0,2,1:T(2,128)S(1)} %dynamic_update_slice.3), channel_id=1, replica_groups=mesh['req'=32,'head'=8] {'req'}, use_global_device_ids=true, to_apply=%region_8.9 | all-reduce | flops 1024 | bytes 8192 | tf_op jit(solution)/shard_map/pmax | solution.py:138
  386.7 0.1 copy.68
  386.9 0.6 gather_fusion.5
  387.5 0.2 fusion.70
  387.7 1.5 scatter_custom_fusion.5
  389.3 2.3 fusion
  391.6 0.1 broadcast.362
  391.8 2.8 scatter_fusion
  394.6 0.8 copy.88
  395.5 0.2 fusion.16
  395.7 203.3 %reduce-scatter.10.cloned.1.call-done = f32[16,2]{1,0:T(8,128)} async-done(((f32[512,2]{1,0:T(8,128)}), f32[16,2]{1,0:T(8,128)}) %reduce-scatter.10.cloned.1.call-update) | async-done | bytes 144
  599.0 0.8 copy.77
  599.8 0.1 fusion.69
  599.9 0.1 copy.69
  600.0 0.1 copy.71
  600.0 214.6 %reduce-scatter.8.cloned.1.call-done = f32[16,256]{1,0:T(8,128)} async-done(((f32[512,256]{1,0:T(8,128)}), f32[16,256]{1,0:T(8,128)}) %reduce-scatter.8.cloned.1.call-update) | async-done | bytes 16400
  814.7 0.7 reshape.564
  815.4 0.1 fusion.37
  815.5 3.0 convolution_convert_fusion.2
  818.5 60.0 %all-reduce.3.cloned.1.call-done = bf16[16,2048]{1,0:T(8,128)(2,1)} async-done(((bf16[16,2048]{1,0:T(8,128)(2,1)}), bf16[16,2048]{1,0:T(8,128)(2,1)}) %all-reduce.3.cloned.1.call-update) | async-done | bytes 65552 | tf_op jit(solution)/shard_map/psum | solution.py:174
  878.5 1.0 fusion.21
  879.5 1.8 fusion.41
  881.3 3.3 convolution_convert_fusion.1
  884.7 62.9 %all-reduce.5.cloned.1.call-done = bf16[16,2048]{1,0:T(8,128)(2,1)} async-done(((bf16[16,2048]{1,0:T(8,128)(2,1)}), bf16[16,2048]{1,0:T(8,128)(2,1)}) %all-reduce.5.cloned.1.call-update) | async-done | bytes 65552 | tf_op jit(solution)/shard_map/psum | solution.py:186
  947.6 1.5 fusion.24
  949.1 2.4 scatter_custom_fusion
  951.6 0.1 dynamic_slice.12
  951.6 77.6 %all-gather.2.cloned.1.call-done = bf16[512,2048]{1,0:T(8,128)(2,1)} async-done(((bf16[16,2048]{1,0:T(8,128)(2,1)}), bf16[512,2048]{1,0:T(8,128)(2,1)}) %all-gather.2.cloned.1.call-update) | async-done | bytes 2097168 | tf_op jit(solution)/shard_map/all_gather | solution.py:188
  1029.2 2.6 convolution_convert_fusion
  (54 shorter events, 0.6 us)
Async XLA Ops:
  6.5 304.4 %copy-start = (bf16[64,128,1,128]{3,1,2,0:T(8,128)(2,1)S(1)}, bf16[64,128,1,128]{3,1,2,0:T(8,128)(2,1)}, u32[]{:S(2)}) copy-start(bf16[64,128,1,128]{3,1,2,0:T(8,128)(2,1)} %param.22) | copy-start | bytes 6291460
  6.5 7.1 copy-start.2
  6.5 6.4 copy-start.1
  6.5 7.1 copy-start.6
  6.5 7.1 copy-start.3
  6.5 592.5 %reduce-scatter.10.cloned.1.call-start = ((), (), s32[]{:S(2)}) async-start(), calls=%async_computation.6 | async-start | bytes 270336
  9.2 5.2 copy-start.10
  12.9 54.3 %copy-start.7 = (s32[512,64]{0,1:T(8,128)S(1)}, s32[512,64]{0,1:T(8,128)}, u32[]{:S(2)}) copy-start(s32[512,64]{0,1:T(8,128)} %param.21) | copy-start | bytes 393220
  309.3 3.9 copy-start.4
  310.9 2.7 copy-start.9
  389.3 425.4 %reduce-scatter.8.cloned.1.call-start = ((), (), s32[]{:S(2)}) async-start(), calls=%async_computation.5 | async-start | bytes 540672
  391.6 3.9 copy-start.5
  395.4 484.1 %copy-start.8 = (f32[2048]{0:T(1024)S(1)}, f32[2048]{0:T(1024)}, u32[]{:S(2)}) copy-start(f32[2048]{0:T(1024)} %param.32) | copy-start | bytes 24580
  395.4 483.1 %all-reduce.3.cloned.1.call-start = ((), (), s32[]{:S(2)}) async-start(), calls=%async_computation.2 | async-start | bytes 131072 | tf_op jit(solution)/shard_map/psum | solution.py:174
  818.5 129.1 %all-reduce.5.cloned.1.call-start = ((), (), s32[]{:S(2)}) async-start(), calls=%async_computation.3 | async-start | bytes 131072 | tf_op jit(solution)/shard_map/psum | solution.py:186
  884.6 144.6 %all-gather.2.cloned.1.call-start = ((), (), s32[]{:S(2)}) async-start(), calls=%async_computation.4 | async-start | bytes 2162688 | tf_op jit(solution)/shard_map/all_gather | solution.py:188
Sparse Core Ops, SparseCore 0:
  389.4 209.5 reduce-scatter.9
  603.3 211.3 reduce-scatter.7
  818.6 59.8 all-reduce.2
  884.7 62.8 all-reduce.4
  950.0 79.1 all-gather.1
where the time goes:
time: 1040 us
  waiting for transfers between devices  619 us (60%)
  local copies, waits for them, and re-layouts  254 us (24%)
  blocking collectives  125 us (12%)
  matrix products  15.3 us (1%)
  between operations  13.5 us (1%)
  other arithmetic  12.2 us (1%)
    unnamed x7, waiting for transfers between devices  418 us
    scatter x1, local copies, waits for them, and re-layouts, body(): jnp.zeros((pool_pages,), jnp.int32).at[targets].set(slot_flat, mode='drop')  120 us
    scatter x1, local copies, waits for them, and re-layouts, body(): jnp.full((pool_pages,), all_rows, jnp.int32).at[targets]  120 us
    all_gather x1, waiting for transfers between devices, body(): lax.all_gather(result, 'req', axis=0, tiled=True)  77.6 us
    pmax x1, blocking collectives, body(): global_peaks = lax.pmax(with_self, 'req')  72.4 us
    psum x1, waiting for transfers between devices, body(): lax.psum(down_part.astype(jnp.bfloat16), 'head').astype(jnp.float32)  62.9 us
    psum x1, waiting for transfers between devices, body(): lax.psum(projected.astype(jnp.bfloat16), 'head').astype(jnp.float32)  60 us
    all_gather x1, blocking collectives, body(): all_queries = lax.all_gather(queries, 'req', axis=0, tiled=True)  52.5 us
  transfers between devices with their start and end apart: 5, of which 5 were waited for; matrix products, arithmetic and copies ran while one was open for 1% of the time, Pallas kernels for 0%

commit v1 on v0

--- a/solution.py
+++ b/solution.py
@@ -90,7 +90,8 @@
         .reshape(local_rows, local_kv, head_width)
     )
     gate_logits = jnp.dot(normed, w_gate, preferred_element_type=jnp.float32)
-    all_queries = lax.all_gather(queries, "req", axis=0, tiled=True)
+    repeated = jnp.stack([queries] * lax.axis_size("req"))
+    all_queries = jnp.concatenate(lax.all_to_all(repeated, "req", 0, 0), axis=0)
     dealt_lengths = lengths[deal_order]
     dealt_tables = page_table[deal_order]
     page_counts = (dealt_lengths + page_size - 1) // page_size

time: 1040 us -> 1000 us (0.962)
  blocking collectives: 125 us -> 74.9 us
  starting transfers between devices: 0.21 us -> 11.8 us
    all_gather x1 -> x0, blocking collectives: 52.5 us -> none  [body(): all_queries = lax.all_gather(queries, 'req', axis=0, tiled=True)]
    all_to_all x0 -> x1, starting transfers between devices: none -> 11.6 us  [body(): all_queries = jnp.concatenate(lax.all_to_all(repeated, 'req', 0, 0), axis=0)]
  transfers between devices with their start and end apart: 5 -> 6, of which waited for: 5 -> 5; matrix products, arithmetic and copies ran while one was open for 1% -> 26% of each run, Pallas kernels for 0% -> 0%
where the time goes in v1:
time: 1000 us
  waiting for transfers between devices  618 us (62%)
  local copies, waits for them, and re-layouts  255 us (26%)
  blocking collectives  74.9 us (7%)
  matrix products  16.5 us (2%)
  between operations  13.6 us (1%)
  starting transfers between devices  11.8 us (1%)
  other arithmetic  11.5 us (1%)
    unnamed x7, waiting for transfers between devices  417 us
    scatter x1, local copies, waits for them, and re-layouts, body(): jnp.zeros((pool_pages,), jnp.int32).at[targets].set(slot_flat, mode='drop')  120 us
    scatter x1, local copies, waits for them, and re-layouts, body(): jnp.full((pool_pages,), all_rows, jnp.int32).at[targets]  120 us
    all_gather x1, waiting for transfers between devices, body(): lax.all_gather(result, 'req', axis=0, tiled=True)  77.6 us
    pmax x1, blocking collectives, body(): global_peaks = lax.pmax(with_self, 'req')  74.9 us
    psum x1, waiting for transfers between devices, body(): lax.psum(down_part.astype(jnp.bfloat16), 'head').astype(jnp.float32)  62.9 us
    psum x1, waiting for transfers between devices, body(): lax.psum(projected.astype(jnp.bfloat16), 'head').astype(jnp.float32)  60 us
  transfers between devices with their start and end apart: 6, of which 5 were waited for; matrix products, arithmetic and copies ran while one was open for 26% of the time, Pallas kernels for 0%

profile of v1, /device:TPU:2, one launch (start us, length us, event | category | flops | bytes accessed | tf_op | source)
XLA Modules:
  0.0 1001.5 jit_solution(5545379389266184666)
XLA Ops:
  6.6 1.1 fusion.17
  7.7 0.8 compare_select_fusion.2
  8.5 1.3 gather_fusion.3
  9.8 1.6 fusion.78
  11.4 0.1 multiply_reduce_fusion
  11.5 0.1 multiply_cosine_fusion.1
  11.7 0.1 multiply_multiply_fusion
  11.7 0.1 fusion.53
  11.8 0.1 pad_maximum_fusion
  11.9 0.8 stack.2
  12.8 11.6 %all-to-all-start = ((bf16[32,16,1,2,128]{4,3,2,1,0:T(2,128)(2,1)}), bf16[32,16,1,2,128]{4,3,2,1,0:T(2,128)(2,1)S(1)}, u32[]{:S(2)}, u32[]{:S(2)}) async-start(bf16[32,16,1,2,128]{4,3,2,1,0:T(2,128)(2,1)} %stack.2), calls=%async_computation | async-start | bytes 524288 | tf_op jit(solution)/shard_map/all_to_all | solution.py:94
  24.5 3.5 gather_fusion
  28.0 0.3 multiply_reduce_fusion.1
  28.5 0.1 fusion.58
  28.6 0.1 maximum_bitcast_fusion
  28.7 0.1 fusion.55
  28.8 0.1 copy.65
  28.9 0.2 iota_compare_fusion
  29.1 0.1 lt.102
  29.2 0.1 copy.57
  29.4 1.0 gather_fusion.1
  30.4 0.2 sub.57
  30.6 0.1 reshape.515
  30.8 0.1 reshape.507
  30.9 0.4 compare_select_fusion
  31.3 120.0 %scatter_custom_fusion.2 = s32[64]{0:T(128)S(1)} fusion(s32[32768]{0:T(1024)S(1)} %bitcast.102, s32[32768]{0:T(1024)S(1)} %reshape.515, s32[]{:T(128)} %constant.24.clone.1), kind=kCustom, calls=%fused_computation.127 | custom fusion | bytes 260 | tf_op jit(solution)/shard_map/scatter | solution.py:109
  151.3 120.0 %scatter_custom_fusion.1 = s32[64]{0:T(128)S(1)} fusion(s32[32768]{0:T(1024)S(1)} %bitcast.103, s32[32768]{0:T(1024)S(1)} %reshape.507, s32[]{:T(128)} %constant.25.clone.1), kind=kCustom, calls=%fused_computation.129 | custom fusion | bytes 260 | tf_op jit(solution)/shard_map/scatter | solution.py:108
  271.4 0.8 gather_fusion.2
  272.2 0.1 iota_compare_fusion.1
  272.3 0.6 gather_fusion.4
  272.9 1.3 fusion.81
  274.2 0.9 scatter_custom_fusion.3
  275.1 0.1 copy.58
  275.2 0.1 copy.59
  275.3 0.1 dynamic_update_slice.3
  275.4 74.9 %pmax.7 = f32[512,1,2]{0,2,1:T(2,128)S(1)} all-reduce(f32[512,1,2]{0,2,1:T(2,128)S(1)} %dynamic_update_slice.3), channel_id=1, replica_groups=mesh['req'=32,'head'=8] {'req'}, use_global_device_ids=true, to_apply=%region_8.9 | all-reduce | flops 1024 | bytes 8192 | tf_op jit(solution)/shard_map/pmax | solution.py:139
  350.3 0.1 copy.60
  350.5 0.6 gather_fusion.5
  351.1 0.2 fusion.71
  351.3 1.5 scatter_custom_fusion.5
  352.9 2.3 fusion
  355.2 0.1 broadcast.364
  355.3 2.8 scatter_fusion
  358.2 0.8 copy.80
  359.1 0.2 fusion.16
  359.3 202.8 %reduce-scatter.10.cloned.1.call-done = f32[16,2]{1,0:T(8,128)} async-done(((f32[512,2]{1,0:T(8,128)}), f32[16,2]{1,0:T(8,128)}) %reduce-scatter.10.cloned.1.call-update) | async-done | bytes 144
  562.2 0.8 copy.69
  562.9 0.1 fusion.70
  563.0 0.1 copy.61
  563.1 0.1 copy.63
  563.2 214.5 %reduce-scatter.8.cloned.1.call-done = f32[16,256]{1,0:T(8,128)} async-done(((f32[512,256]{1,0:T(8,128)}), f32[16,256]{1,0:T(8,128)}) %reduce-scatter.8.cloned.1.call-update) | async-done | bytes 16400
  777.7 0.7 reshape.569
  778.5 0.1 fusion.37
  778.6 3.0 convolution_convert_fusion.2
  781.6 60.0 %all-reduce.3.cloned.1.call-done = bf16[16,2048]{1,0:T(8,128)(2,1)} async-done(((bf16[16,2048]{1,0:T(8,128)(2,1)}), bf16[16,2048]{1,0:T(8,128)(2,1)}) %all-reduce.3.cloned.1.call-update) | async-done | bytes 65552 | tf_op jit(solution)/shard_map/psum | solution.py:175
  841.6 1.0 fusion.21
  842.6 1.8 fusion.41
  844.4 3.3 convolution_convert_fusion.1
  847.8 62.9 %all-reduce.5.cloned.1.call-done = bf16[16,2048]{1,0:T(8,128)(2,1)} async-done(((bf16[16,2048]{1,0:T(8,128)(2,1)}), bf16[16,2048]{1,0:T(8,128)(2,1)}) %all-reduce.5.cloned.1.call-update) | async-done | bytes 65552 | tf_op jit(solution)/shard_map/psum | solution.py:187
  910.7 1.5 fusion.24
  912.2 2.4 scatter_custom_fusion
  914.7 0.1 dynamic_slice.12
  914.7 77.6 %all-gather.2.cloned.1.call-done = bf16[512,2048]{1,0:T(8,128)(2,1)} async-done(((bf16[16,2048]{1,0:T(8,128)(2,1)}), bf16[512,2048]{1,0:T(8,128)(2,1)}) %all-gather.2.cloned.1.call-update) | async-done | bytes 2097168 | tf_op jit(solution)/shard_map/all_gather | solution.py:189
  992.4 2.6 convolution_convert_fusion
  (56 shorter events, 0.6 us)
Async XLA Ops:
  6.5 266.4 %copy-start = (bf16[64,128,1,128]{3,1,2,0:T(8,128)(2,1)S(1)}, bf16[64,128,1,128]{3,1,2,0:T(8,128)(2,1)}, u32[]{:S(2)}) copy-start(bf16[64,128,1,128]{3,1,2,0:T(8,128)(2,1)} %param.22) | copy-start | bytes 6291460
  6.5 17.9 %copy-start.8 = (s32[512]{0:T(512)S(1)}, s32[512]{0:T(512)}, u32[]{:S(2)}) copy-start(s32[512]{0:T(512)} %param.19) | copy-start | bytes 6148
  6.5 17.9 %copy-start.1 = (s32[512]{0:T(512)S(1)}, s32[512]{0:T(512)}, u32[]{:S(2)}) copy-start(s32[512]{0:T(512)} %param.20) | copy-start | bytes 6148
  6.5 5.1 copy-start.10
  11.4 16.6 %copy-start.2 = (bf16[16,2048]{1,0:T(8,128)(2,1)S(1)}, bf16[16,2048]{1,0:T(8,128)(2,1)}, u32[]{:S(2)}) copy-start(bf16[16,2048]{1,0:T(8,128)(2,1)} %param.18) | copy-start | bytes 196612
  11.4 16.6 %copy-start.3 = (bf16[2048,128]{1,0:T(8,128)(2,1)S(1)}, bf16[2048,128]{1,0:T(8,128)(2,1)}, u32[]{:S(2)}) copy-start(bf16[2048,128]{1,0:T(8,128)(2,1)} %param.26) | copy-start | bytes 1572868
  11.4 16.6 %copy-start.5 = (f32[2048]{0:T(1024)S(1)}, f32[2048]{0:T(1024)}, u32[]{:S(2)}) copy-start(f32[2048]{0:T(1024)} %param.24) | copy-start | bytes 24580
  12.8 15.6 %copy-start.9 = (f32[128]{0:T(128)S(1)}, f32[128]{0:T(128)}, u32[]{:S(2)}) copy-start(f32[128]{0:T(128)} %param.31) | copy-start | bytes 1540
  12.8 259.5 %all-to-all-start = ((bf16[32,16,1,2,128]{4,3,2,1,0:T(2,128)(2,1)}), bf16[32,16,1,2,128]{4,3,2,1,0:T(2,128)(2,1)S(1)}, u32[]{:S(2)}, u32[]{:S(2)}) async-start(bf16[32,16,1,2,128]{4,3,2,1,0:T(2,128)(2,1)} %stack.2), calls=%async_computation | async-start | bytes 524288 | tf_op jit(solution)/shard_map/all_to_all | solution.py:94
  24.4 4.8 copy-start.6
  24.4 537.8 %reduce-scatter.10.cloned.1.call-start = ((), (), s32[]{:S(2)}) async-start(), calls=%async_computation.7 | async-start | bytes 270336
  352.8 424.9 %reduce-scatter.8.cloned.1.call-start = ((), (), s32[]{:S(2)}) async-start(), calls=%async_computation.6 | async-start | bytes 540672
  355.2 3.9 copy-start.4
  359.0 483.6 %copy-start.7 = (f32[2048]{0:T(1024)S(1)}, f32[2048]{0:T(1024)}, u32[]{:S(2)}) copy-start(f32[2048]{0:T(1024)} %param.32) | copy-start | bytes 24580
  359.0 482.6 %all-reduce.3.cloned.1.call-start = ((), (), s32[]{:S(2)}) async-start(), calls=%async_computation.3 | async-start | bytes 131072 | tf_op jit(solution)/shard_map/psum | solution.py:175
  781.6 129.1 %all-reduce.5.cloned.1.call-start = ((), (), s32[]{:S(2)}) async-start(), calls=%async_computation.4 | async-start | bytes 131072 | tf_op jit(solution)/shard_map/psum | solution.py:187
  847.7 144.6 %all-gather.2.cloned.1.call-start = ((), (), s32[]{:S(2)}) async-start(), calls=%async_computation.5 | async-start | bytes 2162688 | tf_op jit(solution)/shard_map/all_gather | solution.py:189
Sparse Core Ops, SparseCore 0:
  353.0 209.1 reduce-scatter.9
  566.4 211.2 reduce-scatter.7
  781.7 59.9 all-reduce.2
  847.8 62.8 all-reduce.4
  913.1 79.1 all-gather.1
